TPU v7x, 32 devices: a whole 2x2x4 slice. The times are simulated.
32 devices in a mesh: group: 2 (over y), batch: 4 (over z), mp: 2 (over x), section: 2 (over core).
Axes of the slice: x: 2, y: 2, z: 4, core: 2. Of those that a mesh axis runs over, the one named last changes fastest.
Arguments:
- queries: bfloat16 [2, 192, 8192], P('section', ('group', 'batch'), 'mp'), parts along dimension 1, may hold values from -6 to 6
- new_keys: bfloat16 [2, 192, 1024], P('section', ('group', 'batch'), 'mp'), parts along dimension 1, may hold values from -6 to 6
- new_values: bfloat16 [2, 192, 1024], P('section', ('group', 'batch'), 'mp'), parts along dimension 1, may hold values from -6 to 6
- key_pages: bfloat16 [2, 768, 16, 1024], P('section', ('group', 'batch'), None, 'mp'), parts along dimension 1, may hold values from -6 to 6
- value_pages: bfloat16 [2, 768, 16, 1024], P('section', ('group', 'batch'), None, 'mp'), parts along dimension 1, may hold values from -6 to 6
- page_table: int32 [192, 4], P(('group', 'batch')), parts along dimension 0, may hold values from 0 to 95, as said below
- ancestry: int32 [192], P('group'), parts along dimension 0, may hold values from 0 to 95, as said below
- lengths: int32 [192], P('group'), parts along dimension 0, may hold values from 1 to 64, as said below
- step_rows: bfloat16 [8192, 4096], P(('group', 'batch', 'section'), 'mp'), parts along dimension 0, may hold values from -6 to 6
- norm_gain: float32 [4096], replicated, may hold values from 0.1 to 1.9
- head_weight: bfloat16 [4096, 4096], P(('batch', 'section'), 'mp'), may hold values from -0.09375 to 0.09375
- head_bias: float32 [4096], P('mp'), may hold values from -5 to 5
- class_weight: bfloat16 [4096, 2], P('mp'), may hold values from -0.125 to 0.125
- class_bias: float32 [2], replicated, may hold values from -4 to 4
Outputs:
- attention: bfloat16 [2, 192, 8192], P('section', ('group', 'batch'), 'mp'), parts along dimension 1
- log_odds: float32 [8192], P(('group', 'batch', 'section')), parts along dimension 0
There are 2 independent parts, one for each index of `group`. A program takes and returns all parts, laid end to end along the dimension named above; an argument that names none is the same for every part. Nothing has to cross between parts.
Inputs may be any that keep to these rules, and one draw needn't show every extreme that they name: The pages of the particles on one index of batch lie on that index; the page_table rows of those 24 particles name each of its 96 pages exactly once. Particle j belongs to problem j % 24, and ancestry[j] % 24 == j % 24. Particles j // 24 == d stand on index d of batch; the 24 slots on one index take at most 12 ancestors from any one index, and in every draw some index gives exactly 12 ancestors to the slots of every index. `lengths`: some particle has all 64 positions live in every draw.
All inputs are finite; a program needn't handle non-finite values.
Results may differ from a plain program's by a relative error of at most 0.0043.
Values may be sent and summed in bfloat16 or wider, within the bound.
A program may use at most 64 MiB of HBM per device.

v0:
```python
import jax
import jax.numpy as jnp
from jax import lax
from jax.sharding import PartitionSpec as P

HD = 128


def cache_score_terms(query_head_count, cached_key_rows, cache_values, live_lengths):
    score_scale = 1.0 / HD**0.5
    attention_scores = (
        jnp.einsum(
            "bkgd,btkd->bkgt", query_head_count, cached_key_rows, preferred_element_type=jnp.float32
        )
        * score_scale
    )
    live_mask = jnp.arange(cached_key_rows.shape[1])[None, :] < live_lengths[:, None]
    attention_scores = jnp.where(live_mask[:, None, None, :], attention_scores, -1e30)
    top_score = jnp.max(attention_scores, axis=-1)
    weights = jnp.exp(attention_scores - top_score[..., None])
    denominator = jnp.sum(weights, axis=-1)
    numerator = jnp.einsum(
        "bkgt,btkd->bkgd",
        weights.astype(jnp.bfloat16),
        cache_values,
        preferred_element_type=jnp.float32,
    )
    return (numerator, top_score, denominator)


def finish(numerator, top_score, denominator, query_head_count, particle_key_rows, own_values):
    score_scale = 1.0 / HD**0.5
    own_score = (
        jnp.einsum(
            "vnrc,vnc->vnr", query_head_count, particle_key_rows, preferred_element_type=jnp.float32
        )
        * score_scale
    )
    own_weight = jnp.exp(own_score - top_score)
    result = (numerator + own_weight[..., None] * own_values.astype(jnp.float32)[:, :, None, :]) / (
        denominator + own_weight
    )[..., None]
    return result.astype(jnp.bfloat16)


def per_device(
    queries,
    new_keys,
    new_values,
    key_pages,
    value_pages,
    page_table,
    ancestry,
    lengths,
    step_rows,
    norm_gain,
    head_weight,
    head_bias,
    class_weight,
    class_bias,
):
    layer_count = queries.shape[0]
    slot_count = page_table.shape[0]
    page_count = page_table.shape[1]
    page_size = key_pages.shape[2]
    kv_width = key_pages.shape[3]
    kv_local = kv_width // HD
    group_size = queries.shape[2] // kv_width
    context = page_count * page_size
    device_count = lax.axis_size("batch")
    my_index = lax.axis_index("batch")
    capacity = max(2, (2 * slot_count + device_count - 1) // device_count)
    source = (ancestry // slot_count).reshape(device_count, slot_count)
    positions = jnp.arange(slot_count)
    earlier = positions[None, :] < positions[:, None]
    same_source = source[:, :, None] == source[:, None, :]
    source_rank = jnp.sum(same_source & earlier[None, :, :], axis=2)
    slot_ids = jnp.arange(capacity)
    served = (source == my_index)[:, None, :] & (source_rank[:, None, :] == slot_ids[None, :, None])
    served_slot = jnp.sum(jnp.where(served, positions[None, None, :], 0), axis=2)
    own_source = lax.dynamic_index_in_dim(source, my_index, 0, keepdims=False)
    own_rank = lax.dynamic_index_in_dim(source_rank, my_index, 0, keepdims=False)
    flat_index = own_source * capacity + own_rank
    local_lengths = lax.dynamic_slice_in_dim(lengths, my_index * slot_count, slot_count)
    query_head_count = queries.reshape(layer_count * slot_count, kv_local, group_size, HD)
    particle_key_rows = new_keys.reshape(layer_count * slot_count, kv_local, HD)
    own_values = new_values.reshape(layer_count * slot_count, kv_local, HD)
    served_pages = page_table[served_slot]
    wanted = (own_source[None, None, :] == jnp.arange(device_count)[:, None, None]) & (
        own_rank[None, None, :] == slot_ids[None, :, None]
    )
    request_slot = jnp.sum(jnp.where(wanted, positions[None, None, :], 0), axis=2)
    outgoing_queries = jnp.take(queries, request_slot, axis=1)
    arrived_queries = lax.all_to_all(
        outgoing_queries, "batch", split_axis=1, concat_axis=1, tiled=True
    )
    batch_rows = layer_count * device_count * capacity
    served_heads = arrived_queries.reshape(batch_rows, kv_local, group_size, HD)
    served_keys = key_pages[:, served_pages].reshape(batch_rows, context, kv_local, HD)
    served_values = value_pages[:, served_pages].reshape(batch_rows, context, kv_local, HD)
    served_lengths = jnp.tile(
        jnp.take(local_lengths, served_slot).reshape(device_count * capacity), layer_count
    )
    numerator, top_score, denominator = cache_score_terms(
        served_heads, served_keys, served_values, served_lengths
    )
    numerator = numerator.reshape(layer_count, device_count, capacity, kv_local * group_size * HD)
    top_score = top_score.reshape(layer_count, device_count, capacity, kv_local * group_size)
    denominator = denominator.reshape(layer_count, device_count, capacity, kv_local * group_size)
    returned = (
        lax.all_to_all(numerator, "batch", split_axis=1, concat_axis=1, tiled=True),
        lax.all_to_all(top_score, "batch", split_axis=1, concat_axis=1, tiled=True),
        lax.all_to_all(denominator, "batch", split_axis=1, concat_axis=1, tiled=True),
    )

    def pick_part(received, trailing):
        received = received.reshape((layer_count, device_count * capacity) + trailing)
        return jnp.take(received, flat_index, axis=1).reshape(
            (layer_count * slot_count,) + trailing
        )

    numerator = pick_part(returned[0], (kv_local, group_size, HD))
    top_score = pick_part(returned[1], (kv_local, group_size))
    denominator = pick_part(returned[2], (kv_local, group_size))
    result = finish(
        numerator, top_score, denominator, query_head_count, particle_key_rows, own_values
    )
    attention = result.reshape(layer_count, slot_count, kv_local * group_size * HD)
    full_rows = lax.all_gather(step_rows, "mp", axis=1, tiled=True)
    row_values = full_rows.astype(jnp.float32)
    power = jnp.mean(row_values * row_values, axis=1, keepdims=True)
    normed = (row_values * lax.rsqrt(power + 1e-06) * norm_gain).astype(jnp.bfloat16)
    projected = jnp.dot(
        normed,
        lax.all_gather(head_weight, ("batch", "section"), axis=0, tiled=True),
        preferred_element_type=jnp.float32,
    )
    hidden = jnp.maximum(projected + head_bias, 0.0).astype(jnp.bfloat16)
    partial_logits = jnp.dot(hidden, class_weight, preferred_element_type=jnp.float32)
    logits = lax.psum(partial_logits, "mp") + class_bias
    log_odds = logits[:, 1] - logits[:, 0]
    return (attention, log_odds)


def solution(mesh):
    placed = (
        P("section", ("group", "batch"), "mp"),
        P("section", ("group", "batch"), "mp"),
        P("section", ("group", "batch"), "mp"),
        P("section", ("group", "batch"), None, "mp"),
        P("section", ("group", "batch"), None, "mp"),
        P(("group", "batch"), None),
        P("group"),
        P("group"),
        P(("group", "batch", "section"), "mp"),
        P(),
        P(("batch", "section"), "mp"),
        P("mp"),
        P("mp", None),
        P(),
    )
    return jax.shard_map(
        per_device,
        mesh=mesh,
        in_specs=placed,
        out_specs=(P("section", ("group", "batch"), "mp"), P(("group", "batch", "section"))),
        check_vma=False,
    )
```

profile of v0, /device:TPU:0, one launch (start us, length us, event | category | flops | bytes accessed | tf_op | source)
XLA Modules:
  0.0 253.1 jit_solution(18221568556298894525)
XLA Ops:
  11.1 0.9 select_bitcast_fusion
  12.0 6.3 %all-to-all-start = ((bf16[1,4,12,4096]{3,2,0,1:T(8,128)(2,1)}), bf16[1,4,12,4096]{3,2,0,1:T(8,128)(2,1)}, u32[]{:S(2)}, u32[]{:S(2)}) async-start(bf16[1,4,12,4096]{3,2,0,1:T(8,128)(2,1)} %select_bitcast_fusion), calls=%async_computation | async-start | bytes 1048576 | tf_op jit(solution)/shard_map/all_to_all | solution.py:94
  20.9 2.7 %gather_fusion.3 = bf16[192,16,512]{2,1,0:T(8,128)(2,1)} fusion(bf16[96,16,512]{2,1,0:T(8,128)(2,1)S(1)} %bitcast.71, s32[1024]{0:T(1024)S(1)} %pad_clamp_fusion.2), kind=kCustom, calls=%fused_computation.5 | custom fusion | bytes 6292224 | tf_op jit(solution)/shard_map/gather | solution.py:99
  23.6 5.6 %reshape.355 = bf16[48,64,4,128]{3,2,1,0:T(4,128)(2,1)} reshape(bf16[192,16,512]{2,1,0:T(8,128)(2,1)} %gather_fusion.3) | data formatting | bytes 6291456 | tf_op jit(solution)/shard_map/reshape | solution.py:99
  29.3 3.6 %all-to-all-done = bf16[1,4,12,4096]{3,2,0,1:T(8,128)(2,1)} async-done(((bf16[1,4,12,4096]{3,2,0,1:T(8,128)(2,1)}), bf16[1,4,12,4096]{3,2,0,1:T(8,128)(2,1)}, u32[]{:S(2)}, u32[]{:S(2)}) %all-to-all-start) | async-done | bytes 393248 | tf_op jit(solution)/shard_map/all_to_all | solution.py:94
  33.0 2.1 reshape.354
  35.0 3.9 %fusion.35 = (f32[48,4,8]{2,1,0:T(4,128)S(1)}, f32[48,4,8,64]{3,2,1,0:T(8,128)S(1)}) fusion(bf16[48,4,8,128]{3,2,1,0:T(8,128)(2,1)} %reshape.354, bf16[48,64,4,128]{3,2,1,0:T(4,128)(2,1)} %reshape.355, pred[48,64]{1,0:T(8,128)(4,1)S(1)} %iota_compare_fusion.1), kind=kOutput, calls=%fused_computation.71 | convolution fusion | flops 25459200 | bytes 3941376 | tf_op jit(solution)/shard_map/bkgd,btkd->bkgt/dot_general | solution.py:12
  41.7 1.5 reduce.4
  43.9 3.2 %all-to-all-start.3 = ((f32[4,1,384]{2,1,0:T(1,128)}), f32[4,1,384]{2,1,0:T(1,128)S(1)}, u32[]{:S(2)}, u32[]{:S(2)}) async-start(f32[4,1,384]{2,1,0:T(1,128)} %reshape.484), calls=%async_computation.3 | async-start | bytes 12288 | tf_op jit(solution)/shard_map/all_to_all | solution.py:113
  47.1 2.7 %gather_fusion.4 = bf16[192,16,512]{2,1,0:T(8,128)(2,1)} fusion(bf16[96,16,512]{2,1,0:T(8,128)(2,1)S(1)} %bitcast.74, s32[1024]{0:T(1024)S(1)} %pad_clamp_fusion.2), kind=kCustom, calls=%fused_computation.6 | custom fusion | bytes 6292224 | tf_op jit(solution)/shard_map/gather | solution.py:100
  49.8 5.6 %reshape.356 = bf16[48,64,4,128]{3,2,1,0:T(4,128)(2,1)} reshape(bf16[192,16,512]{2,1,0:T(8,128)(2,1)} %gather_fusion.4) | data formatting | bytes 6291456 | tf_op jit(solution)/shard_map/reshape | solution.py:100
  57.0 5.0 %all-to-all-start.2 = ((f32[4,1,384]{2,1,0:T(1,128)}), f32[4,1,384]{2,1,0:T(1,128)S(1)}, u32[]{:S(2)}, u32[]{:S(2)}) async-start(f32[4,1,384]{2,1,0:T(1,128)} %reshape.482), calls=%async_computation.2 | async-start | bytes 12288 | tf_op jit(solution)/shard_map/all_to_all | solution.py:112
  62.1 3.8 %fusion.9 = f32[48,4,8,128]{3,2,1,0:T(8,128)} fusion(bf16[48,64,4,128]{3,2,1,0:T(4,128)(2,1)} %reshape.356, f32[48,4,8,64]{3,2,1,0:T(8,128)S(1)} %copy-done.4, f32[48,4,8]{2,1,0:T(4,128)S(1)} %get-tuple-element.9), kind=kOutput, calls=%fused_computation.17 | convolution fusion | flops 25362432 | bytes 4331520 | tf_op jit(solution)/shard_map/bkgt,btkd->bkgd/dot_general | solution.py:22
  65.9 1.8 all-to-all-done.2
  67.6 3.7 %all-to-all-start.1 = ((f32[1,4,12,4096]{3,0,2,1:T(1,128)}), f32[1,4,12,4096]{3,0,2,1:T(1,128)S(1)}, u32[]{:S(2)}, u32[]{:S(2)}) async-start(f32[1,4,12,4096]{3,0,2,1:T(1,128)} %bitcast.8), calls=%async_computation.1 | async-start | bytes 1572864 | tf_op jit(solution)/shard_map/all_to_all | solution.py:111
  75.3 0.9 broadcast_multiply_fusion
  76.2 1.1 mul.82
  77.3 27.7 %all-to-all-done.1 = f32[1,4,12,4096]{3,0,2,1:T(1,128)S(1)} async-done(((f32[1,4,12,4096]{3,0,2,1:T(1,128)}), f32[1,4,12,4096]{3,0,2,1:T(1,128)S(1)}, u32[]{:S(2)}, u32[]{:S(2)}) %all-to-all-start.1) | async-done | bytes 786464 | tf_op jit(solution)/shard_map/all_to_all | solution.py:111
  105.0 1.3 gather_fusion.5
  106.4 1.1 gather.38
  108.3 3.2 %fusion = f32[512]{0:T(512)S(1)} fusion(bf16[512,4096]{1,0:T(8,128)(2,1)} %all-gather.3.cloned.1.call-done), kind=kLoop, calls=%fused_computation.10 | loop fusion | flops 6290944 | bytes 4196352 | tf_op jit(solution)/shard_map/reduce_sum | solution.py:131
  111.5 115.2 %all-gather.5.cloned.1.call-done = bf16[4096,2048]{1,0:T(8,128)(2,1)} async-done(((bf16[512,2048]{1,0:T(8,128)(2,1)}), bf16[4096,2048]{1,0:T(8,128)(2,1)}) %all-gather.5.cloned.1.call-update) | async-done | bytes 16777232 | tf_op jit(solution)/shard_map/all_gather | solution.py:135
  226.6 14.0 %fusion.20 = f32[512,2]{0,1:T(2,128)S(1)} fusion(bf16[2048,2]{0,1:T(2,128)(2,1)S(1)} %copy-done.11, bf16[4096,2048]{1,0:T(8,128)(2,1)} %all-gather.5.cloned.1.call-done, bf16[512,4096]{1,0:T(8,128)(2,1)} %all-gather.3.cloned.1.call-done, f32[4096]{0:T(1024)S(1)} %copy-done.10, f32[512]{0:T(512)S(1)} %add_rsqrt_fusion, f32[2048]{0:T(1024)S(1)} %copy-done.12), kind=kOutput, calls=%fused_computation.23 | convolution fusion | flops 8605663232 | bytes 21010432 | tf_op jit(solution)/shard_map/dot_general | solution.py:139
  240.7 4.9 %psum.7 = f32[512,2]{0,1:T(2,128)S(1)} all-reduce(f32[512,2]{0,1:T(2,128)S(1)} %fusion.20), channel_id=1, replica_groups=mesh['group'=2,'batch'=4,'mp'=2,'section'=2] {'mp'}, use_global_device_ids=true, to_apply=%region_6.8 | all-reduce | flops 1024 | bytes 8192 | tf_op jit(solution)/shard_map/psum | solution.py:140
  (102 shorter events, 16.7 us)
Async XLA Ops:
  7.2 13.7 %copy-start = (bf16[1,96,16,512]{3,2,1,0:T(8,128)(2,1)S(1)}, bf16[1,96,16,512]{3,2,1,0:T(8,128)(2,1)}, u32[]{:S(2)}) copy-start(bf16[1,96,16,512]{3,2,1,0:T(8,128)(2,1)} %param.19) | copy-start | bytes 4718596
  7.2 1.5 copy-start.13
  7.2 3.0 %copy-start.1 = (bf16[1,24,4096]{2,1,0:T(8,128)(2,1)S(1)}, bf16[1,24,4096]{2,1,0:T(8,128)(2,1)}, u32[]{:S(2)}) copy-start(bf16[1,24,4096]{2,1,0:T(8,128)(2,1)} %param.16) | copy-start | bytes 589828
  7.2 101.1 %all-gather.3.cloned.1.call-start = ((), (), s32[]{:S(2)}) async-start(), calls=%async_computation.4 | async-start | bytes 6291456 | tf_op jit(solution)/shard_map/all_gather | solution.py:129
  7.9 218.7 %all-gather.5.cloned.1.call-start = ((), (), s32[]{:S(2)}) async-start(), calls=%async_computation.5 | async-start | bytes 18874368 | tf_op jit(solution)/shard_map/all_gather | solution.py:135
  10.2 8.7 %copy-start.7 = (s32[24,4]{0,1:T(4,128)S(1)}, s32[24,4]{0,1:T(4,128)}, u32[]{:S(2)}) copy-start(s32[24,4]{0,1:T(4,128)} %param.21) | copy-start | bytes 1156
  10.2 9.6 %copy-start.14 = (s32[96]{0:T(128)S(1)}, s32[96]{0:T(128)}, u32[]{:S(2)}) copy-start(s32[96]{0:T(128)} %param.23) | copy-start | bytes 1156
  12.0 20.9 %all-to-all-start = ((bf16[1,4,12,4096]{3,2,0,1:T(8,128)(2,1)}), bf16[1,4,12,4096]{3,2,0,1:T(8,128)(2,1)}, u32[]{:S(2)}, u32[]{:S(2)}) async-start(bf16[1,4,12,4096]{3,2,0,1:T(8,128)(2,1)} %select_bitcast_fusion), calls=%async_computation | async-start | bytes 1048576 | tf_op jit(solution)/shard_map/all_to_all | solution.py:94
  29.3 17.8 %copy-start.2 = (bf16[1,96,16,512]{3,2,1,0:T(8,128)(2,1)S(1)}, bf16[1,96,16,512]{3,2,1,0:T(8,128)(2,1)}, u32[]{:S(2)}) copy-start(bf16[1,96,16,512]{3,2,1,0:T(8,128)(2,1)} %param.20) | copy-start | bytes 4718596
  38.9 0.9 copy-start.3
  43.9 13.1 %all-to-all-start.3 = ((f32[4,1,384]{2,1,0:T(1,128)}), f32[4,1,384]{2,1,0:T(1,128)S(1)}, u32[]{:S(2)}, u32[]{:S(2)}) async-start(f32[4,1,384]{2,1,0:T(1,128)} %reshape.484), calls=%async_computation.3 | async-start | bytes 12288 | tf_op jit(solution)/shard_map/all_to_all | solution.py:113
  49.8 12.2 %copy-start.4 = (f32[48,4,8,64]{3,2,1,0:T(8,128)S(1)}, f32[48,4,8,64]{3,2,1,0:T(8,128)}, u32[]{:S(2)}) copy-start(f32[48,4,8,64]{3,2,1,0:T(8,128)} %copy-done.3) | copy-start | bytes 1179652
  57.0 10.6 %all-to-all-start.2 = ((f32[4,1,384]{2,1,0:T(1,128)}), f32[4,1,384]{2,1,0:T(1,128)S(1)}, u32[]{:S(2)}, u32[]{:S(2)}) async-start(f32[4,1,384]{2,1,0:T(1,128)} %reshape.482), calls=%async_computation.2 | async-start | bytes 12288 | tf_op jit(solution)/shard_map/all_to_all | solution.py:112
  62.1 9.3 %copy-start.5 = (bf16[1,24,512]{2,1,0:T(8,128)(2,1)S(1)}, bf16[1,24,512]{2,1,0:T(8,128)(2,1)}, u32[]{:S(2)}) copy-start(bf16[1,24,512]{2,1,0:T(8,128)(2,1)} %param.17) | copy-start | bytes 73732
  62.1 9.3 %copy-start.6 = (bf16[1,24,512]{2,1,0:T(8,128)(2,1)S(1)}, bf16[1,24,512]{2,1,0:T(8,128)(2,1)}, u32[]{:S(2)}) copy-start(bf16[1,24,512]{2,1,0:T(8,128)(2,1)} %param.18) | copy-start | bytes 73732
  62.1 9.4 %copy-start.8 = (s32[24]{0:T(128)S(1)}, s32[24]{0:T(128)}, u32[]{:S(2)}) copy-start(s32[24]{0:T(128)} %get-tuple-element.6) | copy-start | bytes 292
  67.6 37.4 %all-to-all-start.1 = ((f32[1,4,12,4096]{3,0,2,1:T(1,128)}), f32[1,4,12,4096]{3,0,2,1:T(1,128)S(1)}, u32[]{:S(2)}, u32[]{:S(2)}) async-start(f32[1,4,12,4096]{3,0,2,1:T(1,128)} %bitcast.8), calls=%async_computation.1 | async-start | bytes 1572864 | tf_op jit(solution)/shard_map/all_to_all | solution.py:111
  106.4 120.3 %copy-start.10 = (f32[4096]{0:T(1024)S(1)}, f32[4096]{0:T(1024)}, u32[]{:S(2)}) copy-start(f32[4096]{0:T(1024)} %param.25) | copy-start | bytes 49156
  106.4 120.3 %copy-start.11 = (bf16[2048,2]{0,1:T(2,128)(2,1)S(1)}, bf16[2048,2]{0,1:T(2,128)(2,1)}, u32[]{:S(2)}) copy-start(bf16[2048,2]{0,1:T(2,128)(2,1)} %param.28) | copy-start | bytes 24580
  106.4 120.3 %copy-start.12 = (f32[2048]{0:T(1024)S(1)}, f32[2048]{0:T(1024)}, u32[]{:S(2)}) copy-start(f32[2048]{0:T(1024)} %param.27) | copy-start | bytes 24580
  111.5 134.2 %copy-start.9 = (f32[2]{0:T(128)S(1)}, f32[2]{0:T(128)}, u32[]{:S(2)}) copy-start(f32[2]{0:T(128)} %param.29) | copy-start | bytes 28
Sparse Core Ops, SparseCore 0:
  9.6 59.4 all-gather.2
  70.6 155.9 all-gather.4
where the time goes:
time: 254 us; the launch traced here: 253 us
  waiting for transfers between devices  150 us (59%)
  local copies, waits for them, and re-layouts  31.5 us (12%)
  matrix products  21.9 us (9%)
  starting transfers between devices  18.4 us (7%)
  between operations  14.4 us (6%)
  other arithmetic  12.3 us (5%)
  blocking collectives  4.94 us (2%)
    all_gather x1, waiting for transfers between devices, per_device(): lax.all_gather(head_weight, ('batch', 'section'), axis=0, tiled=True)  115 us
    all_to_all x1, waiting for transfers between devices, per_device(): lax.all_to_all(numerator, 'batch', split_axis=1, concat_axis=1, tiled=True)  27.7 us
    dot_general x1, matrix products, per_device(): jnp.dot(hidden, class_weight, preferred_element_type=jnp.float32)  14 us
    all_to_all x1, starting transfers between devices, per_device(): lax.all_to_all(outgoing_queries, 'batch', split_axis=1, concat_axis=1, ti...  6.35 us
    reshape x1, local copies, waits for them, and re-layouts, per_device(): key_pages[:, served_pages].reshape(batch_rows, context, kv_local, HD)  5.62 us
    reshape x1, local copies, waits for them, and re-layouts, per_device(): value_pages[:, served_pages].reshape(batch_rows, context, kv_local, HD)  5.6 us
  transfers between devices with their start and end apart: 6, of which 4 were waited for; matrix products, arithmetic and copies ran while one was open for 20% of the time, Pallas kernels for 0%

commit v1 on v0

--- a/solution.py
+++ b/solution.py
@@ -108,7 +108,12 @@
     top_score = top_score.reshape(layer_count, device_count, capacity, kv_local * group_size)
     denominator = denominator.reshape(layer_count, device_count, capacity, kv_local * group_size)
     returned = (
-        lax.all_to_all(numerator, "batch", split_axis=1, concat_axis=1, tiled=True),
+        jnp.concatenate(
+            lax.all_to_all(
+                jnp.stack(jnp.split(numerator, lax.axis_size("batch"), axis=1)), "batch", 0, 0
+            ),
+            axis=1,
+        ),
         lax.all_to_all(top_score, "batch", split_axis=1, concat_axis=1, tiled=True),
         lax.all_to_all(denominator, "batch", split_axis=1, concat_axis=1, tiled=True),
     )

time: 254 us -> 254 us (level)
  waiting for transfers between devices: 150 us -> 146 us
    all_to_all x1, waiting for transfers between devices: 3.65 us -> 0.01 us  [per_device(): lax.all_to_all(outgoing_queries, 'batch', split_axis=1, concat_axis=1, ti...]
    another operation x0 -> x2, local copies, waits for them, and re-layouts: none -> 2.65 us  [per_device(): jnp.stack(jnp.split(numerator, lax.axis_size('batch'), axis=1))]
  transfers between devices with their start and end apart: 6 -> 6, of which waited for: 4 -> 3; matrix products, arithmetic and copies ran while one was open for 20% -> 21% of each run, Pallas kernels for 0% -> 0%
where the time goes in v1:
time: 254 us; the launch traced here: 253 us
  waiting for transfers between devices  146 us (57%)
  local copies, waits for them, and re-layouts  33.3 us (13%)
  matrix products  21.8 us (9%)
  starting transfers between devices  20.3 us (8%)
  between operations  14.4 us (6%)
  other arithmetic  12 us (5%)
  blocking collectives  4.94 us (2%)
    all_gather x1, waiting for transfers between devices, per_device(): lax.all_gather(head_weight, ('batch', 'section'), axis=0, tiled=True)  114 us
    all_to_all x1, waiting for transfers between devices, per_device(): lax.all_to_all(jnp.stack(jnp.split(numerator, lax.axis_size('batch'), axi...  27.7 us
    dot_general x1, matrix products, per_device(): jnp.dot(hidden, class_weight, preferred_element_type=jnp.float32)  14 us
    all_to_all x1, starting transfers between devices, per_device(): lax.all_to_all(outgoing_queries, 'batch', split_axis=1, concat_axis=1, ti...  6.35 us
    reshape x1, local copies, waits for them, and re-layouts, per_device(): value_pages[:, served_pages].reshape(batch_rows, context, kv_local, HD)  5.75 us
    reshape x1, local copies, waits for them, and re-layouts, per_device(): key_pages[:, served_pages].reshape(batch_rows, context, kv_local, HD)  5.53 us
    all_to_all x1, starting transfers between devices, per_device(): lax.all_to_all(top_score, 'batch', split_axis=1, concat_axis=1, tiled=True)  5.09 us
    all_to_all x1, starting transfers between devices, per_device(): lax.all_to_all(denominator, 'batch', split_axis=1, concat_axis=1, tiled=T...  5.09 us
  transfers between devices with their start and end apart: 6, of which 3 were waited for; matrix products, arithmetic and copies ran while one was open for 21% of the time, Pallas kernels for 0%

profile of v1, /device:TPU:0, one launch (start us, length us, event | category | flops | bytes accessed | tf_op | source)
XLA Modules:
  0.0 253.0 jit_solution(4023877899823016515)
XLA Ops:
  10.6 0.9 select_bitcast_fusion
  11.5 6.3 %all-to-all-start = ((bf16[1,4,12,4096]{3,2,0,1:T(8,128)(2,1)}), bf16[1,4,12,4096]{3,2,0,1:T(8,128)(2,1)}, u32[]{:S(2)}, u32[]{:S(2)}) async-start(bf16[1,4,12,4096]{3,2,0,1:T(8,128)(2,1)} %select_bitcast_fusion), calls=%async_computation | async-start | bytes 1048576 | tf_op jit(solution)/shard_map/all_to_all | solution.py:94
  20.4 2.7 %gather_fusion.4 = bf16[192,16,512]{2,1,0:T(8,128)(2,1)} fusion(bf16[96,16,512]{2,1,0:T(8,128)(2,1)S(1)} %bitcast.80, s32[1024]{0:T(1024)S(1)} %pad_clamp_fusion.2), kind=kCustom, calls=%fused_computation.6 | custom fusion | bytes 6292224 | tf_op jit(solution)/shard_map/gather | solution.py:100
  23.1 5.8 %reshape.353 = bf16[48,64,4,128]{3,2,1,0:T(4,128)(2,1)} reshape(bf16[192,16,512]{2,1,0:T(8,128)(2,1)} %gather_fusion.4) | data formatting | bytes 6291456 | tf_op jit(solution)/shard_map/reshape | solution.py:100
  28.9 2.7 %gather_fusion.3 = bf16[192,16,512]{2,1,0:T(8,128)(2,1)} fusion(bf16[96,16,512]{2,1,0:T(8,128)(2,1)S(1)} %bitcast.83, s32[1024]{0:T(1024)S(1)} %pad_clamp_fusion.2), kind=kCustom, calls=%fused_computation.5 | custom fusion | bytes 6292224 | tf_op jit(solution)/shard_map/gather | solution.py:99
  31.6 5.5 %reshape.352 = bf16[48,64,4,128]{3,2,1,0:T(4,128)(2,1)} reshape(bf16[192,16,512]{2,1,0:T(8,128)(2,1)} %gather_fusion.3) | data formatting | bytes 6291456 | tf_op jit(solution)/shard_map/reshape | solution.py:99
  37.2 1.3 reshape.351
  38.6 3.7 %fusion.35 = (f32[48,4,8]{2,1,0:T(4,128)S(1)}, f32[48,4,8,64]{3,2,1,0:T(8,128)S(1)}) fusion(bf16[48,4,8,128]{3,2,1,0:T(8,128)(2,1)S(1)} %reshape.351, bf16[48,64,4,128]{3,2,1,0:T(4,128)(2,1)} %reshape.352, pred[48,64]{1,0:T(8,128)(4,1)S(1)} %iota_compare_fusion.1), kind=kOutput, calls=%fused_computation.76 | convolution fusion | flops 25459200 | bytes 3941376 | tf_op jit(solution)/shard_map/bkgd,btkd->bkgt/dot_general | solution.py:12
  44.9 5.1 %all-to-all-start.3 = ((f32[4,1,384]{2,1,0:T(1,128)}), f32[4,1,384]{2,1,0:T(1,128)S(1)}, u32[]{:S(2)}, u32[]{:S(2)}) async-start(f32[4,1,384]{2,1,0:T(1,128)} %reshape.480), calls=%async_computation.3 | async-start | bytes 12288 | tf_op jit(solution)/shard_map/all_to_all | solution.py:118
  50.0 3.8 %fusion.9 = f32[48,4,8,128]{3,2,1,0:T(8,128)} fusion(bf16[48,64,4,128]{3,2,1,0:T(4,128)(2,1)} %reshape.353, f32[48,4,8,64]{3,2,1,0:T(8,128)S(1)} %get-tuple-element.14, f32[48,4,8]{2,1,0:T(4,128)S(1)} %get-tuple-element.13), kind=kOutput, calls=%fused_computation.17 | convolution fusion | flops 25362432 | bytes 4331520 | tf_op jit(solution)/shard_map/bkgt,btkd->bkgd/dot_general | solution.py:22
  53.8 1.3 reshape.354
  57.5 5.1 %all-to-all-start.2 = ((f32[4,1,384]{2,1,0:T(1,128)}), f32[4,1,384]{2,1,0:T(1,128)S(1)}, u32[]{:S(2)}, u32[]{:S(2)}) async-start(f32[4,1,384]{2,1,0:T(1,128)} %reshape.478), calls=%async_computation.2 | async-start | bytes 12288 | tf_op jit(solution)/shard_map/all_to_all | solution.py:117
  62.5 1.1 pad_maximum_fusion
  63.6 1.8 copy.60
  65.4 2.7 %all-to-all-done.2 = f32[4,1,384]{2,1,0:T(1,128)S(1)} async-done(((f32[4,1,384]{2,1,0:T(1,128)}), f32[4,1,384]{2,1,0:T(1,128)S(1)}, u32[]{:S(2)}, u32[]{:S(2)}) %all-to-all-start.2) | async-done | bytes 6176 | tf_op jit(solution)/shard_map/all_to_all | solution.py:117
  68.1 3.7 %all-to-all-start.1 = ((f32[4,1,1,12,4096]{4,2,3,1,0:T(1,128)}), f32[4,1,1,12,4096]{4,2,3,1,0:T(1,128)S(1)}, u32[]{:S(2)}, u32[]{:S(2)}) async-start(f32[4,1,1,12,4096]{4,2,3,1,0:T(1,128)} %copy.60), calls=%async_computation.1 | async-start | bytes 1572864 | tf_op jit(solution)/shard_map/all_to_all | solution.py:112
  76.6 1.1 mul.82
  77.7 27.7 %all-to-all-done.1 = f32[4,1,1,12,4096]{4,2,3,1,0:T(1,128)S(1)} async-done(((f32[4,1,1,12,4096]{4,2,3,1,0:T(1,128)}), f32[4,1,1,12,4096]{4,2,3,1,0:T(1,128)S(1)}, u32[]{:S(2)}, u32[]{:S(2)}) %all-to-all-start.1) | async-done | bytes 786464 | tf_op jit(solution)/shard_map/all_to_all | solution.py:112
  105.5 1.3 gather_fusion.5
  106.8 1.3 gather.38
  108.9 3.1 %fusion = f32[512]{0:T(512)S(1)} fusion(bf16[512,4096]{1,0:T(8,128)(2,1)} %all-gather.3.cloned.1.call-done), kind=kLoop, calls=%fused_computation.10 | loop fusion | flops 6290944 | bytes 4196352 | tf_op jit(solution)/shard_map/reduce_sum | solution.py:136
  112.0 114.5 %all-gather.5.cloned.1.call-done = bf16[4096,2048]{1,0:T(8,128)(2,1)} async-done(((bf16[512,2048]{1,0:T(8,128)(2,1)}), bf16[4096,2048]{1,0:T(8,128)(2,1)}) %all-gather.5.cloned.1.call-update) | async-done | bytes 16777232 | tf_op jit(solution)/shard_map/all_gather | solution.py:140
  226.5 14.0 %fusion.20 = f32[512,2]{0,1:T(2,128)S(1)} fusion(bf16[2048,2]{0,1:T(2,128)(2,1)S(1)} %copy-done.8, bf16[4096,2048]{1,0:T(8,128)(2,1)} %all-gather.5.cloned.1.call-done, bf16[512,4096]{1,0:T(8,128)(2,1)} %all-gather.3.cloned.1.call-done, f32[4096]{0:T(1024)S(1)} %copy-done.7, f32[512]{0:T(512)S(1)} %add_rsqrt_fusion, f32[2048]{0:T(1024)S(1)} %copy-done.9), kind=kOutput, calls=%fused_computation.23 | convolution fusion | flops 8605663232 | bytes 21010432 | tf_op jit(solution)/shard_map/dot_general | solution.py:144
  240.6 4.9 %psum.7 = f32[512,2]{0,1:T(2,128)S(1)} all-reduce(f32[512,2]{0,1:T(2,128)S(1)} %fusion.20), channel_id=1, replica_groups=mesh['group'=2,'batch'=4,'mp'=2,'section'=2] {'mp'}, use_global_device_ids=true, to_apply=%region_6.8 | all-reduce | flops 1024 | bytes 8192 | tf_op jit(solution)/shard_map/psum | solution.py:145
  (100 shorter events, 17.0 us)
Async XLA Ops:
  7.2 13.2 %copy-start = (bf16[1,96,16,512]{3,2,1,0:T(8,128)(2,1)S(1)}, bf16[1,96,16,512]{3,2,1,0:T(8,128)(2,1)}, u32[]{:S(2)}) copy-start(bf16[1,96,16,512]{3,2,1,0:T(8,128)(2,1)} %param.20) | copy-start | bytes 4718596
  7.2 1.5 copy-start.10
  7.2 2.5 copy-start.1
  7.2 101.7 %all-gather.3.cloned.1.call-start = ((), (), s32[]{:S(2)}) async-start(), calls=%async_computation.4 | async-start | bytes 6291456 | tf_op jit(solution)/shard_map/all_gather | solution.py:134
  7.9 218.6 %all-gather.5.cloned.1.call-start = ((), (), s32[]{:S(2)}) async-start(), calls=%async_computation.5 | async-start | bytes 18874368 | tf_op jit(solution)/shard_map/all_gather | solution.py:140
  9.7 8.7 %copy-start.5 = (s32[24,4]{0,1:T(4,128)S(1)}, s32[24,4]{0,1:T(4,128)}, u32[]{:S(2)}) copy-start(s32[24,4]{0,1:T(4,128)} %param.21) | copy-start | bytes 1156
  9.7 9.6 %copy-start.11 = (s32[96]{0:T(128)S(1)}, s32[96]{0:T(128)}, u32[]{:S(2)}) copy-start(s32[96]{0:T(128)} %param.23) | copy-start | bytes 1156
  11.5 25.7 %all-to-all-start = ((bf16[1,4,12,4096]{3,2,0,1:T(8,128)(2,1)}), bf16[1,4,12,4096]{3,2,0,1:T(8,128)(2,1)}, u32[]{:S(2)}, u32[]{:S(2)}) async-start(bf16[1,4,12,4096]{3,2,0,1:T(8,128)(2,1)} %select_bitcast_fusion), calls=%async_computation | async-start | bytes 1048576 | tf_op jit(solution)/shard_map/all_to_all | solution.py:94
  23.1 5.8 %copy-start.2 = (bf16[1,96,16,512]{3,2,1,0:T(8,128)(2,1)S(1)}, bf16[1,96,16,512]{3,2,1,0:T(8,128)(2,1)}, u32[]{:S(2)}) copy-start(bf16[1,96,16,512]{3,2,1,0:T(8,128)(2,1)} %param.19) | copy-start | bytes 4718596
  44.9 12.5 %all-to-all-start.3 = ((f32[4,1,384]{2,1,0:T(1,128)}), f32[4,1,384]{2,1,0:T(1,128)S(1)}, u32[]{:S(2)}, u32[]{:S(2)}) async-start(f32[4,1,384]{2,1,0:T(1,128)} %reshape.480), calls=%async_computation.3 | async-start | bytes 12288 | tf_op jit(solution)/shard_map/all_to_all | solution.py:118
  55.9 15.9 %copy-start.3 = (bf16[1,24,512]{2,1,0:T(8,128)(2,1)S(1)}, bf16[1,24,512]{2,1,0:T(8,128)(2,1)}, u32[]{:S(2)}) copy-start(bf16[1,24,512]{2,1,0:T(8,128)(2,1)} %param.17) | copy-start | bytes 73732
  55.9 15.9 %copy-start.4 = (bf16[1,24,512]{2,1,0:T(8,128)(2,1)S(1)}, bf16[1,24,512]{2,1,0:T(8,128)(2,1)}, u32[]{:S(2)}) copy-start(bf16[1,24,512]{2,1,0:T(8,128)(2,1)} %param.18) | copy-start | bytes 73732
  57.5 10.7 %all-to-all-start.2 = ((f32[4,1,384]{2,1,0:T(1,128)}), f32[4,1,384]{2,1,0:T(1,128)S(1)}, u32[]{:S(2)}, u32[]{:S(2)}) async-start(f32[4,1,384]{2,1,0:T(1,128)} %reshape.478), calls=%async_computation.2 | async-start | bytes 12288 | tf_op jit(solution)/shard_map/all_to_all | solution.py:117
  68.1 37.3 %all-to-all-start.1 = ((f32[4,1,1,12,4096]{4,2,3,1,0:T(1,128)}), f32[4,1,1,12,4096]{4,2,3,1,0:T(1,128)S(1)}, u32[]{:S(2)}, u32[]{:S(2)}) async-start(f32[4,1,1,12,4096]{4,2,3,1,0:T(1,128)} %copy.60), calls=%async_computation.1 | async-start | bytes 1572864 | tf_op jit(solution)/shard_map/all_to_all | solution.py:112
  106.8 119.7 %copy-start.7 = (f32[4096]{0:T(1024)S(1)}, f32[4096]{0:T(1024)}, u32[]{:S(2)}) copy-start(f32[4096]{0:T(1024)} %param.25) | copy-start | bytes 49156
  106.8 119.7 %copy-start.8 = (bf16[2048,2]{0,1:T(2,128)(2,1)S(1)}, bf16[2048,2]{0,1:T(2,128)(2,1)}, u32[]{:S(2)}) copy-start(bf16[2048,2]{0,1:T(2,128)(2,1)} %param.28) | copy-start | bytes 24580
  106.8 119.7 %copy-start.9 = (f32[2048]{0:T(1024)S(1)}, f32[2048]{0:T(1024)}, u32[]{:S(2)}) copy-start(f32[2048]{0:T(1024)} %param.27) | copy-start | bytes 24580
  112.0 133.5 %copy-start.6 = (f32[2]{0:T(128)S(1)}, f32[2]{0:T(128)}, u32[]{:S(2)}) copy-start(f32[2]{0:T(128)} %param.29) | copy-start | bytes 28
Sparse Core Ops, SparseCore 0:
  9.6 59.4 all-gather.2
  70.6 155.8 all-gather.4
